TPU v7x, 32 devices: a whole 2x2x4 slice. The times are simulated.
32 devices in a mesh: row: 8 (over y, x, core), col: 4 (over z).
Axes of the slice: x: 2, y: 2, z: 4, core: 2. Of those that a mesh axis runs over, the one named last changes fastest.
Arguments:
- pair_in: bfloat16 [384, 384, 128], P('row', 'col'), may hold values from -6 to 6
- coords: float32 [3, 384], P(None, 'row'), may hold values from -36 to 36
- chain_ids: int32 [384], P('row'), may hold values from 0 to 3, never falling along the last dimension, each value on 1 to 192 neighbouring positions
- coord_mask: int32 [384], P('row'), may hold values 0 or 1
- gain_tri: float32 [128], replicated, may hold values from 0.1 to 1.9
- gain_sum: float32 [128], replicated, may hold values from 0.1 to 1.9
- gain_attn: float32 [128], replicated, may hold values from 0.1 to 1.9
- w_tri_in: bfloat16 [128, 640], replicated, may hold values from -0.5 to 0.5
- w_tri_out: bfloat16 [128, 128], replicated, may hold values from -0.5 to 0.5
- w_bins: float32 [36, 128], replicated, may hold values from -3 to 3
- same_chain: float32 [128], replicated, may hold values from -6 to 6
- w_query: bfloat16 [128, 128], replicated, may hold values from -8 to 8
- w_attn: bfloat16 [128, 384], replicated, may hold values from -0.5 to 0.5
- w_bias: bfloat16 [128, 4], replicated, may hold values from -0.5 to 0.5
- w_attn_out: bfloat16 [128, 128], replicated, may hold values from -0.5 to 0.5
Outputs:
- pair_out: bfloat16 [384, 384, 128], P('row', 'col')
Inputs may be any that keep to these rules, and one draw needn't show every extreme that they name: `chain_ids`: chain numbers never fall along the residues, and no chain holds more than half of them.
All inputs are finite; a program needn't handle non-finite values. No bound on the sum of `coord_mask` on one device may be relied on, other than what follows from the above.
Results may differ from a plain program's by a relative error of at most 0.02.
Values may be sent and summed in bfloat16 or wider, within the bound.
A program may use at most 192 MiB of HBM per device.

v0:
```python
import math
import jax
import jax.numpy as jnp
from jax import lax
from jax.sharding import PartitionSpec as P


def layer_norm(values, gain):
    center = values - jnp.mean(values, axis=-1, keepdims=True)
    spread = jnp.mean(center * center, axis=-1, keepdims=True)
    return center * lax.rsqrt(spread + 1e-05) * gain


def body(
    pair_in,
    coords,
    chain_ids,
    coord_mask,
    gain_tri,
    gain_sum,
    gain_attn,
    w_tri_in,
    w_tri_out,
    w_bins,
    same_chain,
    w_query,
    w_attn,
    w_bias,
    w_attn_out,
):
    row_count, col_count, channels = pair_in.shape
    n_heads = w_bias.shape[1]
    head_size = channels // n_heads
    n_bins = w_bins.shape[0]
    col_start = lax.axis_index("col") * col_count
    coords_all, chains_all, masks_all = (
        lax.all_gather(coords, "row", axis=1, tiled=True),
        lax.all_gather(chain_ids, "row", axis=0, tiled=True),
        lax.all_gather(coord_mask, "row", axis=0, tiled=True),
    )
    pair_wide = pair_in.astype(jnp.float32)
    normed = layer_norm(pair_wide, gain_tri).astype(jnp.bfloat16)
    projected = jnp.dot(
        normed.reshape(row_count * col_count, channels),
        w_tri_in,
        preferred_element_type=jnp.float32,
    ).reshape(row_count, col_count, 5 * channels)
    left_side = (
        (jax.nn.sigmoid(projected[..., :channels]) * projected[..., channels : 2 * channels])
        .astype(jnp.bfloat16)
        .transpose(2, 0, 1)
    )
    right_side = (
        (
            jax.nn.sigmoid(projected[..., 2 * channels : 3 * channels])
            * projected[..., 3 * channels : 4 * channels]
        )
        .astype(jnp.bfloat16)
        .transpose(2, 0, 1)
    )
    tri_gate = jax.nn.sigmoid(projected[..., 4 * channels :])
    right_cols = lax.all_gather(right_side, "row", axis=1, tiled=True)
    summed = lax.psum_scatter(
        jnp.einsum("cjk,cik->jci", right_cols, left_side, preferred_element_type=jnp.float32),
        "col",
        scatter_dimension=0,
        tiled=True,
    )
    product = summed.transpose(2, 0, 1)
    summed_norm = layer_norm(product, gain_sum).astype(jnp.bfloat16)
    pair_one = pair_wide + tri_gate * jnp.dot(
        summed_norm.reshape(row_count * col_count, channels),
        w_tri_out,
        preferred_element_type=jnp.float32,
    ).reshape(row_count, col_count, channels)
    far_coords = lax.dynamic_slice_in_dim(coords_all, col_start, col_count, 1)
    far_chains = lax.dynamic_slice_in_dim(chains_all, col_start, col_count, 0)
    far_masks = lax.dynamic_slice_in_dim(masks_all, col_start, col_count, 0)
    offsets = coords[:, :, None] - far_coords[:, None, :]
    dist = jnp.sqrt(jnp.sum(offsets * offsets, axis=0) + 1.0)
    centres = 2.0 + 20.0 * jnp.arange(n_bins, dtype=jnp.float32) / (n_bins - 1)
    spacing = 25.0 / (n_bins - 1)
    pair_mask = coord_mask.astype(jnp.float32)[:, None] * far_masks.astype(jnp.float32)[None, :]
    feats = jnp.exp(-(((dist[..., None] - centres) / spacing) ** 2)) * pair_mask[..., None]
    binned = jnp.dot(
        feats.reshape(row_count * col_count, n_bins), w_bins, precision=lax.Precision.HIGHEST
    ).reshape(row_count, col_count, channels)
    shared = (chain_ids[:, None] == far_chains[None, :]).astype(jnp.float32)
    pair_two = (pair_one + binned + shared[..., None] * same_chain).astype(jnp.bfloat16)
    normed_two = layer_norm(pair_two.astype(jnp.float32), gain_attn).astype(jnp.bfloat16)
    flat_two = normed_two.reshape(row_count * col_count, channels)
    queries = (
        jnp.dot(flat_two, w_query, preferred_element_type=jnp.float32)
        .astype(jnp.bfloat16)
        .reshape(row_count, col_count, n_heads, head_size)
    )
    gate_pre = jnp.dot(
        flat_two, w_attn[:, 2 * channels :], preferred_element_type=jnp.float32
    ).reshape(row_count, col_count, channels)
    attn_gate = jax.nn.sigmoid(gate_pre)
    pair_bias = (
        jnp.dot(flat_two, w_bias, preferred_element_type=jnp.float32)
        .astype(jnp.bfloat16)
        .reshape(row_count, col_count, n_heads)
        .transpose(2, 0, 1)
    )
    bias_wide = lax.all_gather(pair_bias, "col", axis=2, tiled=True)
    bias_full = lax.all_gather(bias_wide, "row", axis=1, tiled=True)
    bias_mine = lax.dynamic_slice_in_dim(bias_full, col_start, col_count, 1)
    group = math.gcd(row_count, 8)
    blocks = row_count // group
    query_groups = queries.reshape(blocks, group, col_count, n_heads, head_size)
    root_dim = math.sqrt(head_size)
    start_state = (
        jnp.full((blocks, group, n_heads, col_count), -1e30, jnp.float32),
        jnp.zeros((blocks, group, n_heads, col_count), jnp.float32),
        jnp.zeros((blocks, group, n_heads, col_count, head_size), jnp.float32),
    )
    panel = lax.all_gather(normed_two, "col", axis=1, tiled=True)
    span = panel.shape[1]
    both = jnp.dot(
        panel.reshape(row_count * span, channels),
        w_attn[:, : 2 * channels],
        preferred_element_type=jnp.float32,
    ).reshape(row_count, span, 2 * channels)
    key_part = both[..., :channels].astype(jnp.bfloat16)
    span = key_part.shape[1]
    bias_part = bias_mine.astype(jnp.float32)
    key_groups = key_part.reshape(blocks, group, span, n_heads, head_size)
    value_groups = (
        both[..., channels:].astype(jnp.bfloat16).reshape(blocks, group, span, n_heads, head_size)
    )

    def one_block(items):
        query_blk, key_blk, value_blk, running_top, running_total, running_acc = items
        scores = (
            jnp.einsum("ijhd,ikhd->ihjk", query_blk, key_blk, preferred_element_type=jnp.float32)
            / root_dim
            + bias_part[None]
        )
        new_top = jnp.maximum(running_top, jnp.max(scores, axis=-1))
        rescale = jnp.exp(running_top - new_top)
        expo = jnp.exp(scores - new_top[..., None])
        new_total = running_total * rescale + jnp.sum(expo, axis=-1)
        new_acc = running_acc * rescale[..., None] + jnp.einsum(
            "ihjk,ikhd->ihjd",
            expo.astype(jnp.bfloat16),
            value_blk,
            preferred_element_type=jnp.float32,
        )
        return (new_top, new_total, new_acc)

    final_top, final_total, final_acc = lax.map(
        one_block,
        (query_groups, key_groups, value_groups, start_state[0], start_state[1], start_state[2]),
    )
    attended = (
        (final_acc / final_total[..., None])
        .reshape(row_count, n_heads, col_count, head_size)
        .transpose(0, 2, 1, 3)
        .reshape(row_count, col_count, channels)
    )
    gated = (attn_gate * attended).astype(jnp.bfloat16)
    result = pair_two.astype(jnp.float32) + jnp.dot(
        gated.reshape(row_count * col_count, channels),
        w_attn_out,
        preferred_element_type=jnp.float32,
    ).reshape(row_count, col_count, channels)
    return result.astype(jnp.bfloat16)


def solution(mesh):
    return jax.shard_map(
        body,
        mesh=mesh,
        in_specs=(
            P("row", "col", None),
            P(None, "row"),
            P("row"),
            P("row"),
            P(),
            P(),
            P(),
            P(),
            P(),
            P(),
            P(),
            P(),
            P(),
            P(),
            P(),
        ),
        out_specs=P("row", "col", None),
        check_vma=False,
    )
```

profile of v0, /device:TPU:0, one launch (start us, length us, event | category | flops | bytes accessed | tf_op | source)
XLA Modules:
  0.0 504.3 jit_solution(13640466424140914236)
XLA Ops:
  8.4 2.7 fusion.29
  13.2 2.7 fusion.57
  18.9 60.5 %all-gather.5.cloned.1.call-done = bf16[128,384,96]{0,2,1:T(8,128)(2,1)} async-done(((bf16[128,48,96]{0,2,1:T(8,128)(2,1)}), bf16[128,384,96]{0,2,1:T(8,128)(2,1)}) %all-gather.5.cloned.1.call-update) | async-done | bytes 9437200 | tf_op jit(solution)/shard_map/all_gather | solution.py:62
  79.4 15.5 %copy.76 = bf16[128,384,96]{2,1,0:T(8,128)(2,1)} copy(bf16[128,384,96]{0,2,1:T(8,128)(2,1)} %all-gather.5.cloned.1.call-done) | data formatting | bytes 18874368 | tf_op jit(solution)/shard_map/all_gather | solution.py:62
  95.0 13.6 %convolution_bitcast_fusion = f32[384,128,48]{0,2,1:T(8,128)} fusion(bf16[128,48,96]{2,1,0:T(8,128)(2,1)S(1)} %copy.75, bf16[128,384,96]{2,1,0:T(8,128)(2,1)} %copy.76), kind=kOutput, calls=%fused_computation.31 | convolution fusion | flops 452984832 | bytes 20054016 | tf_op jit(solution)/shard_map/cjk,cik->jci/dot_general | solution.py:64
  108.5 9.8 %copy.77 = f32[384,128,48]{1,2,0:T(8,128)} copy(f32[384,128,48]{0,2,1:T(8,128)} %convolution_bitcast_fusion) | data formatting | bytes 18874368 | tf_op jit(solution)/shard_map/cjk,cik->jci/transpose | solution.py:64
  119.0 8.9 %all-gather = f32[8,48,3]{1,2,0:T(4,128)S(1)} all-gather(f32[1,48,3]{1,2,0:T(4,128)S(1)} %bitcast.98), channel_id=1, replica_groups=mesh['row'=8,'col'=4] {'row'}, dimensions={0}, use_global_device_ids=true | all-gather | bytes 5184 | tf_op jit(solution)/shard_map/all_gather | solution.py:37
  129.7 7.0 %all-reduce.2 = (s32[384]{0:T(512)S(1)}, s32[384]{0:T(512)S(1)}) all-reduce(s32[384]{0:T(512)S(1)} %dynamic-update-slice.1, s32[384]{0:T(512)S(1)} %dynamic-update-slice), channel_id=1, replica_groups=mesh['row'=8,'col'=4] {'row'}, use_global_device_ids=true, to_apply=%add.1 | all-reduce | flops 768 | bytes 6144
  137.2 142.5 %reduce-scatter.2.cloned.1.call-done = f32[96,128,48]{1,2,0:T(8,128)} async-done(((f32[384,128,48]{1,2,0:T(8,128)}), f32[96,128,48]{1,2,0:T(8,128)}) %reduce-scatter.2.cloned.1.call-update) | async-done | bytes 2359312 | tf_op jit(solution)/shard_map/reduce_scatter | solution.py:63
  279.7 2.5 bitcast_reduce_fusion
  286.8 7.1 %convert_reduce_fusion = (f32[48,96]{1,0:T(8,128)S(1)}, bf16[48,96,128]{2,1,0:T(8,128)(2,1)S(1)}) fusion(f32[128]{0:T(128)S(1)} %copy-done.20, f32[48,96]{1,0:T(8,128)S(1)} %compare_convert_fusion, f32[36,128]{1,0:T(8,128)S(1)} %copy-done.18, f32[48,96]{1,0:T(8,128)S(1)} %get-tuple-element.114, f32[36]{0:T(128)S(1)} %multiply_add_fusion.1, ...), kind=kOutput, calls=%fused_computation.27 | convolution fusion | flops 262706688 | bytes 7170704 | tf_op jit(solution)/shard_map/dot_general | solution.py:85
  297.8 15.3 %all_gather.26 = bf16[4,48,384]{1,0,2:T(4,128)(2,1)S(1)} all-gather(bf16[4,48,96]{1,0,2:T(4,128)(2,1)S(1)} %bitcast.97), channel_id=1, replica_groups=mesh['row'=8,'col'=4] {'col'}, dimensions={2}, use_global_device_ids=true | all-gather | bytes 184320 | tf_op jit(solution)/shard_map/all_gather | solution.py:107
  318.5 20.2 %all-gather.9.cloned.1.call-done = bf16[4,384,384]{2,0,1:T(4,128)(2,1)} async-done(((bf16[4,48,384]{2,0,1:T(4,128)(2,1)}), bf16[4,384,384]{2,0,1:T(4,128)(2,1)}) %all-gather.9.cloned.1.call-update) | async-done | bytes 1179664 | tf_op jit(solution)/shard_map/all_gather | solution.py:108
  339.8 89.8 %all-gather.7.cloned.1.call-done = bf16[48,384,128]{2,1,0:T(8,128)(2,1)} async-done(((bf16[48,96,128]{2,1,0:T(8,128)(2,1)}), bf16[48,384,128]{2,1,0:T(8,128)(2,1)}) %all-gather.7.cloned.1.call-update) | async-done | bytes 4718608 | tf_op jit(solution)/shard_map/all_gather | solution.py:119
  429.6 8.6 %convolution_convert_fusion = bf16[48,384,256]{1,2,0:T(8,128)(2,1)} fusion(bf16[48,384,128]{2,1,0:T(8,128)(2,1)} %all-gather.7.cloned.1.call-done, bf16[128,384]{1,0:T(8,128)(2,1)} %param.29), kind=kOutput, calls=%fused_computation.22 | convolution fusion | flops 1212678144 | bytes 14221312 | tf_op jit(solution)/shard_map/dot_general | solution.py:121
  438.2 9.3 %fusion.82 = (bf16[48,384,128]{1,2,0:T(8,128)(2,1)}, bf16[48,384,128]{1,2,0:T(8,128)(2,1)}) fusion(bf16[48,384,256]{1,2,0:T(8,128)(2,1)} %convolution_convert_fusion), kind=kLoop, calls=%fused_computation.112 | loop fusion | bytes 18874368 | tf_op jit(solution)/shard_map/slice | solution.py:131
  447.4 41.3 %while.12 = (s32[]{:T(128)}, f32[6,8,4,96]{3,2,1,0:T(4,128)S(1)}, f32[6,8,4,96,32]{3,4,2,1,0:T(8,128)}, bf16[6,8,96,4,32]{2,1,0,4,3:T(8,128)(2,1)S(1)}, bf16[6,8...) while((s32[]{:T(128)}, f32[6,8,4,96]{3,2,1,0:T(4,128)S(1)}, ...), condition=%wide.region_11.12_spmd, body=%wide.region_8.11_spmd.sunk | while | flops 164084736 | bytes 18761308 | solution.py:153
  449.6 3.1 fusion.99
  456.4 3.1 fusion.99
  463.3 3.1 fusion.99
  470.2 3.1 fusion.99
  477.1 3.1 fusion.99
  484.0 3.1 fusion.99
  493.3 4.4 fusion.35
  (128 shorter events, 50.8 us)
Async XLA Ops:
  6.5 4.6 copy-start
  6.5 4.6 copy-start.5
  6.5 4.6 copy-start.12
  6.5 72.9 %all-gather.5.cloned.1.call-start = ((), (), s32[]{:S(2)}) async-start(), calls=%async_computation.1 | async-start | bytes 10616832 | tf_op jit(solution)/shard_map/all_gather | solution.py:62
  13.2 4.6 copy-start.2
  17.9 261.8 %reduce-scatter.2.cloned.1.call-start = ((), (), s32[]{:S(2)}) async-start(), calls=%async_computation.2 | async-start | bytes 11796480 | tf_op jit(solution)/shard_map/reduce_scatter | solution.py:63
  118.3 9.6 %copy-start.19 = (s32[48]{0:T(128)S(1)}, s32[48]{0:T(128)}, u32[]{:S(2)}) copy-start(s32[48]{0:T(128)} %param.20) | copy-start | bytes 580
  118.3 9.6 %copy-start.21 = (u32[32]{0:T(128)S(1)}, u32[32]{0:T(128)}, u32[]{:S(2)}) copy-start(u32[32]{0:T(128)} %constant.69) | copy-start | bytes 388
  118.3 11.1 %copy-start.13 = (s32[48]{0:T(128)S(1)}, s32[48]{0:T(128)}, u32[]{:S(2)}) copy-start(s32[48]{0:T(128)} %param.19) | copy-start | bytes 580
  118.4 220.4 %all-gather.9.cloned.1.call-start = ((), (), s32[]{:S(2)}) async-start(), calls=%async_computation.4 | async-start | bytes 1327104 | tf_op jit(solution)/shard_map/all_gather | solution.py:108
  137.2 146.8 %copy-start.16 = (f32[128]{0:T(128)S(1)}, f32[128]{0:T(128)}, u32[]{:S(2)}) copy-start(f32[128]{0:T(128)} %param.22) | copy-start | bytes 1540
  279.7 2.7 copy-start.3
  283.8 1.7 copy-start.8
  285.5 1.3 copy-start.6
  285.5 1.3 copy-start.18
  286.8 8.8 %copy-start.14 = (f32[128]{0:T(128)S(1)}, f32[128]{0:T(128)}, u32[]{:S(2)}) copy-start(f32[128]{0:T(128)} %param.23) | copy-start | bytes 1540
  293.9 1.7 copy-start.7
  293.9 3.2 copy-start.11
  297.1 17.2 %copy-start.4 = (bf16[48,96,128]{2,1,0:T(8,128)(2,1)}, bf16[48,96,128]{2,1,0:T(8,128)(2,1)S(1)}, u32[]{:S(2)}) copy-start(bf16[48,96,128]{2,1,0:T(8,128)(2,1)S(1)} %fusion.28) | copy-start | bytes 3538948
  297.1 17.5 %copy-start.9 = (bf16[128,128]{1,0:T(8,128)(2,1)S(1)}, bf16[128,128]{1,0:T(8,128)(2,1)}, u32[]{:S(2)}) copy-start(bf16[128,128]{1,0:T(8,128)(2,1)} %param.28) | copy-start | bytes 98308
  314.0 115.6 %all-gather.7.cloned.1.call-start = ((), (), s32[]{:S(2)}) async-start(), calls=%async_computation.3 | async-start | bytes 5898240 | tf_op jit(solution)/shard_map/all_gather | solution.py:119
  491.1 2.2 copy-start.15
  491.1 2.2 copy-start.17
  493.3 4.4 copy-start.1
  (2 other events, 1.9 us)
Sparse Core Ops, SparseCore 0:
  18.0 61.4 all-gather.4
  118.5 161.1 reduce-scatter.1
  314.1 24.5 all-gather.8
  340.1 89.3 all-gather.6
where the time goes:
time: 506 us; the launch traced here: 504 us
  waiting for transfers between devices  313 us (62%)
  matrix products  69.3 us (14%)
  local copies, waits for them, and re-layouts  46.4 us (9%)
  blocking collectives  31.1 us (6%)
  other arithmetic  29.3 us (6%)
  between operations  14.2 us (3%)
    reduce_scatter x1, waiting for transfers between devices, body(): lax.psum_scatter(jnp.einsum('cjk,cik->jci', right_cols, left_side, prefer...  142 us
    all_gather x1, waiting for transfers between devices, body(): panel = lax.all_gather(normed_two, 'col', axis=1, tiled=True)  89.8 us
    all_gather x1, waiting for transfers between devices, body(): right_cols = lax.all_gather(right_side, 'row', axis=1, tiled=True)  60.5 us
    all_gather x1, waiting for transfers between devices, body(): bias_full = lax.all_gather(bias_wide, 'row', axis=1, tiled=True)  20.2 us
    dot_general x6, matrix products, one_block(): jnp.einsum('ihjk,ikhd->ihjd', expo.astype(jnp.bfloat16), value_blk, prefe...  18.7 us
    all_gather x1, local copies, waits for them, and re-layouts, body(): right_cols = lax.all_gather(right_side, 'row', axis=1, tiled=True)  15.5 us
    all_gather x1, blocking collectives, body(): bias_wide = lax.all_gather(pair_bias, 'col', axis=2, tiled=True)  15.3 us
    dot_general x1, matrix products, body(): jnp.einsum('cjk,cik->jci', right_cols, left_side, preferred_element_type=...  13.6 us
  transfers between devices with their start and end apart: 4, of which 4 were waited for; matrix products, arithmetic and copies ran while one was open for 2% of the time, Pallas kernels for 0%

commit v1 on v0

--- a/solution.py
+++ b/solution.py
@@ -3,6 +3,32 @@
 import jax.numpy as jnp
 from jax import lax
 from jax.sharding import PartitionSpec as P
+
+
+def work_both_ways(x, axis, dim, work, out_dim):
+    size, index, rows = (lax.axis_size(axis), lax.axis_index(axis), x.shape[dim])
+    right = [(i, (i + 1) % size) for i in range(size)]
+    left = [(b, a) for a, b in right]
+    lower, upper = (lax.ppermute(x, axis, right), lax.ppermute(x, axis, left))
+    made = work(x, index * rows)
+    length = made.shape[out_dim]
+    result = jnp.zeros(
+        (*made.shape[:out_dim], size * length, *made.shape[out_dim + 1 :]), made.dtype
+    )
+
+    def put(result, made, source):
+        return lax.dynamic_update_slice_in_dim(result, made, source * length, axis=out_dim)
+
+    result = put(result, made, index)
+    for hop in range(1, size // 2 + 1):
+        below, above = ((index - hop) % size, (index + hop) % size)
+        block = (lower, upper)
+        if hop < size // 2:
+            lower, upper = (lax.ppermute(lower, axis, right), lax.ppermute(upper, axis, left))
+        result = put(result, work(block[0], below * rows), below)
+        if 2 * hop < size:
+            result = put(result, work(block[1], above * rows), above)
+    return result
 
 
 def layer_norm(values, gain):
@@ -59,9 +85,16 @@
         .transpose(2, 0, 1)
     )
     tri_gate = jax.nn.sigmoid(projected[..., 4 * channels :])
-    right_cols = lax.all_gather(right_side, "row", axis=1, tiled=True)
     summed = lax.psum_scatter(
-        jnp.einsum("cjk,cik->jci", right_cols, left_side, preferred_element_type=jnp.float32),
+        work_both_ways(
+            right_side,
+            "row",
+            1,
+            lambda own_block, at: jnp.einsum(
+                "cjk,cik->jci", own_block, left_side, preferred_element_type=jnp.float32
+            ),
+            0,
+        ),
         "col",
         scatter_dimension=0,
         tiled=True,

time: 506 us -> 544 us (1.075); the launches traced: 504 us -> 535 us
  waiting for transfers between devices: 313 us -> 273 us
  local copies, waits for them, and re-layouts: 46.4 us -> 85.7 us
  matrix products: 69.3 us -> 88.8 us
  starting transfers between devices: 0.35 us -> 9.43 us
    all_gather x1 -> x0, waiting for transfers between devices: 60.5 us -> none  [body(): right_cols = lax.all_gather(right_side, 'row', axis=1, tiled=True)]
    ppermute x0 -> x7, waiting for transfers between devices: none -> 19.5 us  [the longest x2 19.5 us: work_both_ways(): lower, upper = (lax.ppermute(x, axis, right), lax.ppermute(x, axis, left))]
    ppermute x0 -> x7, local copies, waits for them, and re-layouts: none -> 19.5 us  [the longest x3 8.34 us: work_both_ways(): lax.ppermute(lower, axis, right)]
    dot_general x1 -> x8, matrix products: 13.6 us -> 32 us  [body(): jnp.einsum('cjk,cik->jci', own_block, left_side, preferred_element_type=j...]
    transpose x1 -> x9, local copies, waits for them, and re-layouts: 9.79 us -> 27.5 us  [the longest x8 24.8 us: body(): jnp.einsum('cjk,cik->jci', own_block, left_side, preferred_element_type=j...]
    all_gather x1 -> x0, local copies, waits for them, and re-layouts: 15.5 us -> none  [body(): right_cols = lax.all_gather(right_side, 'row', axis=1, tiled=True)]
    dynamic_update_slice x0 -> x8, local copies, waits for them, and re-layouts: none -> 13.1 us  [put(): lax.dynamic_update_slice_in_dim(result, made, source * length, axis=out_dim)]
    ppermute x0 -> x7, starting transfers between devices: none -> 9.13 us  [the longest x2 4.73 us: work_both_ways(): lax.ppermute(upper, axis, left)]
  transfers between devices with their start and end apart: 4 -> 10, of which waited for: 4 -> 4; matrix products, arithmetic and copies ran while one was open for 2% -> 18% of each run, Pallas kernels for 0% -> 0%
where the time goes in v1:
time: 544 us; the launch traced here: 535 us
  waiting for transfers between devices  273 us (50%)
  matrix products  88.8 us (16%)
  local copies, waits for them, and re-layouts  85.7 us (16%)
  blocking collectives  34.2 us (6%)
  other arithmetic  28.7 us (5%)
  between operations  14.5 us (3%)
  starting transfers between devices  9.43 us (2%)
    reduce_scatter x1, waiting for transfers between devices, body(): lax.psum_scatter(work_both_ways(right_side, 'row', 1, lambda own_block, a...  143 us
    all_gather x1, waiting for transfers between devices, body(): panel = lax.all_gather(normed_two, 'col', axis=1, tiled=True)  89.9 us
    dot_general x8, matrix products, body(): jnp.einsum('cjk,cik->jci', own_block, left_side, preferred_element_type=j...  32 us
    transpose x8, local copies, waits for them, and re-layouts, body(): jnp.einsum('cjk,cik->jci', own_block, left_side, preferred_element_type=j...  24.8 us
    all_gather x1, waiting for transfers between devices, body(): bias_full = lax.all_gather(bias_wide, 'row', axis=1, tiled=True)  20 us
    ppermute x2, waiting for transfers between devices, work_both_ways(): lower, upper = (lax.ppermute(x, axis, right), lax.ppermute(x, axis, left))  19.5 us
    dot_general x6, matrix products, one_block(): jnp.einsum('ihjk,ikhd->ihjd', expo.astype(jnp.bfloat16), value_blk, prefe...  18.8 us
    all_gather x1, blocking collectives, body(): bias_wide = lax.all_gather(pair_bias, 'col', axis=2, tiled=True)  15.3 us
  transfers between devices with their start and end apart: 10, of which 4 were waited for; matrix products, arithmetic and copies ran while one was open for 18% of the time, Pallas kernels for 0%

profile of v1, /device:TPU:0, one launch (start us, length us, event | category | flops | bytes accessed | tf_op | source)
XLA Modules:
  0.0 534.9 jit_solution(11310360852232249790)
XLA Ops:
  26.4 19.5 %collective-permute-done = bf16[128,48,96]{0,2,1:T(8,128)(2,1)} collective-permute-done((bf16[128,48,96]{0,2,1:T(8,128)(2,1)}, bf16[128,48,96]{0,2,1:T(8,128)(2,1)}, u32[]{:S(2)}, u32[]{:S(2)}) %collective-permute-start) | collective-permute-done | bytes 1179680 | tf_op jit(solution)/shard_map/ppermute | solution.py:12
  46.5 4.0 convolution_bitcast_fusion.7
  55.7 4.7 broadcast_in_dim.6
  64.3 4.0 convolution_bitcast_fusion.6
  74.3 4.0 convolution_bitcast_fusion.5
  78.3 3.2 copy.143
  91.0 4.0 convolution_bitcast_fusion.4
  100.9 4.0 convolution_bitcast_fusion.3
  104.9 3.2 copy.149
  114.6 4.0 convolution_bitcast_fusion.2
  124.5 4.0 convolution_bitcast_fusion.1
  128.5 3.2 copy.155
  138.2 4.0 convolution_bitcast_fusion
  146.4 11.4 %all-gather = f32[8,48,3]{1,2,0:T(4,128)S(1)} all-gather(f32[1,48,3]{1,2,0:T(4,128)S(1)} %bitcast.127), channel_id=1, replica_groups=mesh['row'=8,'col'=4] {'row'}, dimensions={0}, use_global_device_ids=true | all-gather | bytes 5184 | tf_op jit(solution)/shard_map/all_gather | solution.py:63
  159.7 7.6 %all-reduce.2 = (s32[384]{0:T(512)S(1)}, s32[384]{0:T(512)S(1)}) all-reduce(s32[384]{0:T(512)S(1)} %dynamic-update-slice.1, s32[384]{0:T(512)S(1)} %dynamic-update-slice), channel_id=1, replica_groups=mesh['row'=8,'col'=4] {'row'}, use_global_device_ids=true, to_apply=%add.1 | all-reduce | flops 768 | bytes 6144
  167.7 143.4 %reduce-scatter.2.cloned.1.call-done = f32[96,128,48]{1,0,2:T(8,128)} async-done(((f32[384,128,48]{1,0,2:T(8,128)}), f32[96,128,48]{1,0,2:T(8,128)}) %reduce-scatter.2.cloned.1.call-update) | async-done | bytes 2359312 | tf_op jit(solution)/shard_map/reduce_scatter | solution.py:88
  317.0 7.0 %convert_reduce_fusion = (f32[48,96]{1,0:T(8,128)S(1)}, bf16[48,96,128]{2,1,0:T(8,128)(2,1)S(1)}) fusion(f32[128]{0:T(128)S(1)} %copy-done.23, f32[48,96]{1,0:T(8,128)S(1)} %compare_convert_fusion, f32[36,128]{1,0:T(8,128)S(1)} %copy-done.21, f32[48,96]{1,0:T(8,128)S(1)} %get-tuple-element.107, f32[36]{0:T(128)S(1)} %multiply_add_fusion.1, ...), kind=kOutput, calls=%fused_computation.27 | convolution fusion | flops 262706688 | bytes 7170704 | tf_op jit(solution)/shard_map/dot_general | solution.py:118
  328.0 15.3 %all_gather.22 = bf16[4,48,384]{1,0,2:T(4,128)(2,1)S(1)} all-gather(bf16[4,48,96]{1,0,2:T(4,128)(2,1)S(1)} %bitcast.126), channel_id=1, replica_groups=mesh['row'=8,'col'=4] {'col'}, dimensions={2}, use_global_device_ids=true | all-gather | bytes 184320 | tf_op jit(solution)/shard_map/all_gather | solution.py:140
  348.8 20.0 %all-gather.6.cloned.1.call-done = bf16[4,384,384]{2,0,1:T(4,128)(2,1)} async-done(((bf16[4,48,384]{2,0,1:T(4,128)(2,1)}), bf16[4,384,384]{2,0,1:T(4,128)(2,1)}) %all-gather.6.cloned.1.call-update) | async-done | bytes 1179664 | tf_op jit(solution)/shard_map/all_gather | solution.py:141
  370.0 89.9 %all-gather.4.cloned.1.call-done = bf16[48,384,128]{2,1,0:T(8,128)(2,1)} async-done(((bf16[48,96,128]{2,1,0:T(8,128)(2,1)}), bf16[48,384,128]{2,1,0:T(8,128)(2,1)}) %all-gather.4.cloned.1.call-update) | async-done | bytes 4718608 | tf_op jit(solution)/shard_map/all_gather | solution.py:152
  459.9 8.6 %convolution_convert_fusion = bf16[48,384,256]{1,2,0:T(8,128)(2,1)} fusion(bf16[48,384,128]{2,1,0:T(8,128)(2,1)} %all-gather.4.cloned.1.call-done, bf16[128,384]{1,0:T(8,128)(2,1)} %param.29), kind=kOutput, calls=%fused_computation.22 | convolution fusion | flops 1212678144 | bytes 14221312 | tf_op jit(solution)/shard_map/dot_general | solution.py:154
  468.5 9.2 %fusion.85 = (bf16[48,384,128]{1,2,0:T(8,128)(2,1)}, bf16[48,384,128]{1,2,0:T(8,128)(2,1)}) fusion(bf16[48,384,256]{1,2,0:T(8,128)(2,1)} %convolution_convert_fusion), kind=kLoop, calls=%fused_computation.130 | loop fusion | bytes 18874368 | tf_op jit(solution)/shard_map/slice | solution.py:164
  477.7 41.3 %while.12 = (s32[]{:T(128)}, f32[6,8,4,96]{3,2,1,0:T(4,128)S(1)}, f32[6,8,4,96,32]{3,4,2,1,0:T(8,128)}, bf16[6,8,96,4,32]{2,1,0,4,3:T(8,128)(2,1)S(1)}, bf16[6,8...) while((s32[]{:T(128)}, f32[6,8,4,96]{3,2,1,0:T(4,128)S(1)}, ...), condition=%wide.region_11.12_spmd, body=%wide.region_8.11_spmd.sunk | while | flops 164084736 | bytes 18761308 | solution.py:186
  523.7 4.5 fusion.35
  (170 shorter events, 137.4 us)
Async XLA Ops:
  6.5 4.6 copy-start
  6.5 4.6 copy-start.5
  6.5 4.6 copy-start.15
  6.5 304.6 %reduce-scatter.2.cloned.1.call-start = ((), (), s32[]{:S(2)}) async-start(), calls=%async_computation.1 | async-start | bytes 11796480 | tf_op jit(solution)/shard_map/reduce_scatter | solution.py:88
  13.2 5.0 copy-start.2
  18.3 27.6 %collective-permute-start = (bf16[128,48,96]{0,2,1:T(8,128)(2,1)}, bf16[128,48,96]{0,2,1:T(8,128)(2,1)}, u32[]{:S(2)}, u32[]{:S(2)}) collective-permute-start(bf16[128,48,96]{0,2,1:T(8,128)(2,1)} %get-tuple-element.100), channel_id=1, source_target_pairs={{0,4},{4,8},{8,12},{12,16},{16,20},{20,24},{24,28},{28,0},{1,5},{5... | collective-permute-start | bytes 3538952 | tf_op jit(solution)/shard_map/ppermute | solution.py:12
  18.8 34.9 %collective-permute-start.1 = (bf16[128,48,96]{0,2,1:T(8,128)(2,1)}, bf16[128,48,96]{0,2,1:T(8,128)(2,1)}, u32[]{:S(2)}, u32[]{:S(2)}) collective-permute-start(bf16[128,48,96]{0,2,1:T(8,128)(2,1)} %get-tuple-element.100), channel_id=1, source_target_pairs={{4,0},{8,4},{12,8},{16,12},{20,16},{24,20},{28,24},{0,28},{5,1},{9... | collective-permute-start | bytes 3538952 | tf_op jit(solution)/shard_map/ppermute | solution.py:12
  45.9 35.6 %collective-permute-start.2 = (bf16[128,48,96]{0,2,1:T(8,128)(2,1)}, bf16[128,48,96]{0,2,1:T(8,128)(2,1)}, u32[]{:S(2)}, u32[]{:S(2)}) collective-permute-start(bf16[128,48,96]{0,2,1:T(8,128)(2,1)} %collective-permute-done), channel_id=1, source_target_pairs={{0,4},{4,8},{8,12},{12,16},{16,20},{20,24},{24,28},{28,0},{1,5},{5... | collective-permute-start | bytes 3538952 | tf_op jit(solution)/shard_map/ppermute | solution.py:27
  53.7 6.7 %copy-start.6 = (f32[48,128,48]{1,0,2:T(8,128)S(1)}, f32[48,128,48]{1,0,2:T(8,128)}, u32[]{:S(2)}) copy-start(f32[48,128,48]{1,0,2:T(8,128)} %copy.137) | copy-start | bytes 3538948
  53.7 34.6 %collective-permute-start.3 = (bf16[128,48,96]{0,2,1:T(8,128)(2,1)}, bf16[128,48,96]{0,2,1:T(8,128)(2,1)}, u32[]{:S(2)}, u32[]{:S(2)}) collective-permute-start(bf16[128,48,96]{0,2,1:T(8,128)(2,1)} %collective-permute-done.1), channel_id=1, source_target_pairs={{4,0},{8,4},{12,8},{16,12},{20,16},{24,20},{28,24},{0,28},{5,1},{9... | collective-permute-start | bytes 3538952 | tf_op jit(solution)/shard_map/ppermute | solution.py:27
  81.5 29.2 %collective-permute-start.4 = (bf16[128,48,96]{0,2,1:T(8,128)(2,1)}, bf16[128,48,96]{0,2,1:T(8,128)(2,1)}, u32[]{:S(2)}, u32[]{:S(2)}) collective-permute-start(bf16[128,48,96]{0,2,1:T(8,128)(2,1)} %collective-permute-done.2), channel_id=1, source_target_pairs={{0,4},{4,8},{8,12},{12,16},{16,20},{20,24},{24,28},{28,0},{1,5},{5... | collective-permute-start | bytes 3538952 | tf_op jit(solution)/shard_map/ppermute | solution.py:27
  88.3 33.5 %collective-permute-start.5 = (bf16[128,48,96]{0,2,1:T(8,128)(2,1)}, bf16[128,48,96]{0,2,1:T(8,128)(2,1)}, u32[]{:S(2)}, u32[]{:S(2)}) collective-permute-start(bf16[128,48,96]{0,2,1:T(8,128)(2,1)} %collective-permute-done.3), channel_id=1, source_target_pairs={{4,0},{8,4},{12,8},{16,12},{20,16},{24,20},{28,24},{0,28},{5,1},{9... | collective-permute-start | bytes 3538952 | tf_op jit(solution)/shard_map/ppermute | solution.py:27
  110.7 24.7 %collective-permute-start.6 = (bf16[128,48,96]{0,2,1:T(8,128)(2,1)}, bf16[128,48,96]{0,2,1:T(8,128)(2,1)}, u32[]{:S(2)}, u32[]{:S(2)}) collective-permute-start(bf16[128,48,96]{0,2,1:T(8,128)(2,1)} %collective-permute-done.4), channel_id=1, source_target_pairs={{0,4},{4,8},{8,12},{12,16},{16,20},{20,24},{24,28},{28,0},{1,5},{5... | collective-permute-start | bytes 3538952 | tf_op jit(solution)/shard_map/ppermute | solution.py:27
  145.7 12.2 %copy-start.22 = (s32[48]{0:T(128)S(1)}, s32[48]{0:T(128)}, u32[]{:S(2)}) copy-start(s32[48]{0:T(128)} %param.20) | copy-start | bytes 580
  145.7 12.2 %copy-start.24 = (u32[32]{0:T(128)S(1)}, u32[32]{0:T(128)}, u32[]{:S(2)}) copy-start(u32[32]{0:T(128)} %constant.128) | copy-start | bytes 388
  145.7 13.7 %copy-start.17 = (s32[48]{0:T(128)S(1)}, s32[48]{0:T(128)}, u32[]{:S(2)}) copy-start(s32[48]{0:T(128)} %param.19) | copy-start | bytes 580
  145.8 223.1 %all-gather.6.cloned.1.call-start = ((), (), s32[]{:S(2)}) async-start(), calls=%async_computation.3 | async-start | bytes 1327104 | tf_op jit(solution)/shard_map/all_gather | solution.py:141
  167.7 147.9 %copy-start.11 = (bf16[128,128]{1,0:T(8,128)(2,1)S(1)}, bf16[128,128]{1,0:T(8,128)(2,1)}, u32[]{:S(2)}) copy-start(bf16[128,128]{1,0:T(8,128)(2,1)} %param.25) | copy-start | bytes 98308
  167.7 147.9 %copy-start.16 = (f32[128]{0:T(128)S(1)}, f32[128]{0:T(128)}, u32[]{:S(2)}) copy-start(f32[128]{0:T(128)} %param.22) | copy-start | bytes 1540
  317.0 8.8 %copy-start.18 = (f32[128]{0:T(128)S(1)}, f32[128]{0:T(128)}, u32[]{:S(2)}) copy-start(f32[128]{0:T(128)} %param.23) | copy-start | bytes 1540
  327.3 17.2 %copy-start.4 = (bf16[48,96,128]{2,1,0:T(8,128)(2,1)}, bf16[48,96,128]{2,1,0:T(8,128)(2,1)S(1)}, u32[]{:S(2)}) copy-start(bf16[48,96,128]{2,1,0:T(8,128)(2,1)S(1)} %fusion.28) | copy-start | bytes 3538948
  327.3 17.6 %copy-start.12 = (bf16[128,128]{1,0:T(8,128)(2,1)S(1)}, bf16[128,128]{1,0:T(8,128)(2,1)}, u32[]{:S(2)}) copy-start(bf16[128,128]{1,0:T(8,128)(2,1)} %param.28) | copy-start | bytes 98308
  344.2 115.7 %all-gather.4.cloned.1.call-start = ((), (), s32[]{:S(2)}) async-start(), calls=%async_computation.2 | async-start | bytes 5898240 | tf_op jit(solution)/shard_map/all_gather | solution.py:152
  523.7 4.5 copy-start.1
  (11 other events, 23.5 us)
Sparse Core Ops, SparseCore 0:
  145.9 165.2 reduce-scatter.1
  344.3 24.5 all-gather.5
  370.4 89.3 all-gather.3
